TPU v7x, 128 devices: a whole 4x4x4 slice. The times are simulated.
128 devices in a mesh: gx: 8 (over z_lo, x), gy: 4 (over z_hi, core), gz: 4 (over y).
Axes of the slice: x: 4, y: 4, z: 4 (z_hi: 2, z_lo: 2; z = z_hi * 2 + z_lo), core: 2. Of those that a mesh axis runs over, the one named last changes fastest.
Arguments:
- x_saved: bfloat16 [1024, 16384], P('gx', ('gy', 'gz')), may hold values from -0.1875 to 0.1875
- grad_out: bfloat16 [1024, 28672], P('gx', ('gz', 'gy')), may hold values from -6 to 6
- weight: bfloat16 [16384, 28672], P('gy', ('gz', 'gx')), may hold values from -0.09375 to 0.09375
Outputs:
- grad_in: bfloat16 [1024, 16384], P('gx', ('gy', 'gz'))
- grad_weight: bfloat16 [16384, 28672], P('gy', ('gz', 'gx'))
All inputs are finite; a program needn't handle non-finite values.
Results may differ from a plain program's by a relative error of at most 0.001.
Values may be sent and summed in bfloat16 or wider, within the bound.
A program may use at most 128 MiB of HBM per device.

v0:
```python
import jax
import jax.numpy as jnp
from jax import lax
from jax.sharding import PartitionSpec as P


def body(x_saved, grad_out, weight):
    token_rows = x_saved.shape[0]
    token_groups = lax.axis_size("gx")
    feature_groups = lax.axis_size("gz")
    grad_block = lax.all_gather(grad_out, "gy", axis=1, tiled=True)
    grad_all = lax.all_to_all(grad_block, "gx", split_axis=1, concat_axis=0, tiled=True)
    unit_cols = grad_all.shape[1]
    inputs_block = lax.all_gather(x_saved, "gz", axis=1, tiled=True)
    summed = jnp.einsum(
        "td,tc->dc",
        lax.all_gather(inputs_block, "gx", axis=0, tiled=True),
        grad_all,
        preferred_element_type=jnp.float32,
    )
    grad_weight = summed.astype(jnp.bfloat16)
    grad_split = grad_all.reshape(token_groups, token_rows, unit_cols)
    weight_split = weight.reshape(feature_groups, weight.shape[0] // feature_groups, unit_cols)
    terms = jnp.einsum(
        "atc,bkc->abtk", grad_split, weight_split, preferred_element_type=jnp.float32
    )
    terms = terms.reshape(token_groups * feature_groups * token_rows, weight_split.shape[1])
    grad_in = lax.psum_scatter(terms, ("gx", "gz"), scatter_dimension=0, tiled=True)
    return (grad_in.astype(jnp.bfloat16), grad_weight)


def solution(mesh):
    return jax.shard_map(
        body,
        mesh=mesh,
        in_specs=(P("gx", ("gy", "gz")), P("gx", ("gz", "gy")), P("gy", ("gz", "gx"))),
        out_specs=(P("gx", ("gy", "gz")), P("gy", ("gz", "gx"))),
        check_vma=False,
    )
```

profile of v0, /device:TPU:0, one launch (start us, length us, event | category | flops | bytes accessed | tf_op | source)
XLA Modules:
  0.0 386.5 jit_solution(9099532467425328987)
XLA Ops:
  7.2 0.0 all-gather.6.cloned.1.call-start
  7.2 0.7 all-gather.6.cloned.1.call-update
  7.9 0.0 all-gather.4.cloned.1.call-start
  7.9 2.0 copy.5
  9.9 0.0 all-gather.4.cloned.1.call-update
  10.0 0.0 all-gather.8.cloned.1.call-start
  10.0 26.1 %all-gather.6.cloned.1.call-done = bf16[128,4096]{1,0:T(8,128)(2,1)} async-done(((bf16[128,1024]{1,0:T(8,128)(2,1)}), bf16[128,4096]{1,0:T(8,128)(2,1)}) %all-gather.6.cloned.1.call-update) | async-done | bytes 1048592 | tf_op jit(solution)/shard_map/all_gather | solution.py:14
  36.1 0.0 all-gather.8.cloned.1.call-update
  36.2 0.0 reduce-scatter.2.cloned.1.call-start
  36.2 27.8 %all-gather.4.cloned.1.call-done = bf16[128,7168]{0,1:T(8,128)(2,1)} async-done(((bf16[128,1792]{0,1:T(8,128)(2,1)}), bf16[128,7168]{0,1:T(8,128)(2,1)}) %all-gather.4.cloned.1.call-update) | async-done | bytes 1835024 | tf_op jit(solution)/shard_map/all_gather | solution.py:11
  64.0 3.1 copy.6
  67.1 46.1 %all_to_all.19 = bf16[128,8,896]{2,0,1:T(8,128)(2,1)S(1)} all-to-all(bf16[128,8,896]{2,0,1:T(8,128)(2,1)S(1)} %copy.6), channel_id=1, replica_groups=mesh['gx'=8,'gy'=4,'gz'=4] {'gx'}, dimensions={1} | all-to-all | bytes 3670016 | tf_op jit(solution)/shard_map/all_to_all | solution.py:12
  113.2 0.0 copy-start
  113.2 11.8 %convolution_bitcast_fusion = f32[8,4,128,1024]{3,2,0,1:T(8,128)S(1)} fusion(bf16[4,1024,896,1]{2,1,3,0:T(8,128)(2,1)} %bitcast.22, bf16[128,8,896]{2,0,1:T(8,128)(2,1)S(1)} %all_to_all.19), kind=kOutput, calls=%fused_computation | convolution fusion | flops 7516192768 | bytes 25952256 | tf_op jit(solution)/shard_map/atc,bkc->abtk/dot_general | solution.py:24
  125.0 0.0 copy-done
  125.0 6.1 %copy.7 = f32[8,4,128,1024]{3,2,1,0:T(8,128)} copy(f32[8,4,128,1024]{3,2,0,1:T(8,128)S(1)} %convolution_bitcast_fusion) | data formatting | bytes 33554432 | tf_op jit(solution)/shard_map/atc,bkc->abtk/transpose | solution.py:24
  131.1 0.0 copy-start.1
  131.1 0.0 reduce-scatter.2.cloned.1.call-update
  131.1 43.9 %all-gather.8.cloned.1.call-done = bf16[1024,4096]{1,0:T(8,128)(2,1)} async-done(((bf16[128,4096]{1,0:T(8,128)(2,1)}), bf16[1024,4096]{1,0:T(8,128)(2,1)}) %all-gather.8.cloned.1.call-update) | async-done | bytes 8388624 | tf_op jit(solution)/shard_map/all_gather | solution.py:17
  175.0 0.0 copy-done.1
  175.1 14.2 %convolution_convert_fusion = bf16[4096,896]{1,0:T(8,128)(2,1)} fusion(bf16[1024,4096]{1,0:T(8,128)(2,1)} %all-gather.8.cloned.1.call-done, bf16[1024,896]{1,0:T(8,128)(2,1)S(1)} %bitcast.21), kind=kOutput, calls=%fused_computation.1 | convolution fusion | flops 7519862784 | bytes 17563648 | tf_op jit(solution)/shard_map/td,tc->dc/dot_general | solution.py:15
  189.3 189.0 %reduce-scatter.2.cloned.1.call-done = f32[128,1024]{1,0:T(8,128)} async-done(((f32[4096,1024]{1,0:T(8,128)}), f32[128,1024]{1,0:T(8,128)}) %reduce-scatter.2.cloned.1.call-update) | async-done | bytes 524304 | tf_op jit(solution)/shard_map/reduce_scatter | solution.py:28
  378.2 1.8 convert_element_type.6
Async XLA Ops:
  7.2 29.0 %all-gather.6.cloned.1.call-start = ((), (), s32[]{:S(2)}) async-start(), calls=%async_computation.4 | async-start | bytes 1310720 | tf_op jit(solution)/shard_map/all_gather | solution.py:14
  7.9 56.1 %all-gather.4.cloned.1.call-start = ((), (), s32[]{:S(2)}) async-start(), calls=%async_computation.2 | async-start | bytes 2293760 | tf_op jit(solution)/shard_map/all_gather | solution.py:11
  10.0 165.1 %all-gather.8.cloned.1.call-start = ((), (), s32[]{:S(2)}) async-start(), calls=%async_computation.5 | async-start | bytes 9437184 | tf_op jit(solution)/shard_map/all_gather | solution.py:17
  36.2 342.1 %reduce-scatter.2.cloned.1.call-start = ((), (), s32[]{:S(2)}) async-start(), calls=%async_computation.3 | async-start | bytes 17301504 | tf_op jit(solution)/shard_map/reduce_scatter | solution.py:28
  113.2 11.8 %copy-start = (bf16[128,8,896]{2,0,1:T(8,128)(2,1)}, bf16[128,8,896]{2,0,1:T(8,128)(2,1)S(1)}, u32[]{:S(2)}) copy-start(bf16[128,8,896]{2,0,1:T(8,128)(2,1)S(1)} %all_to_all.19) | copy-start | bytes 5505028
  131.1 43.9 %copy-start.1 = (bf16[128,8,896]{2,0,1:T(8,128)(2,1)S(1)}, bf16[128,8,896]{2,0,1:T(8,128)(2,1)}, u32[]{:S(2)}) copy-start(bf16[128,8,896]{2,0,1:T(8,128)(2,1)} %copy-done) | copy-start | bytes 5505028
Sparse Core Ops, SparseCore 0:
  9.7 26.4 all-gather.5
  38.4 25.6 all-gather.3
  65.7 109.3 all-gather.7
  177.3 200.8 reduce-scatter.1
where the time goes:
time: 387 us
  waiting for transfers between devices  288 us (74%)
  blocking collectives  46.1 us (12%)
  matrix products  26 us (7%)
  between operations  13.8 us (4%)
  local copies, waits for them, and re-layouts  11.2 us (3%)
    reduce_scatter x1, waiting for transfers between devices, body(): lax.psum_scatter(terms, ('gx', 'gz'), scatter_dimension=0, tiled=True)  189 us
    all_to_all x1, blocking collectives, body(): lax.all_to_all(grad_block, 'gx', split_axis=1, concat_axis=0, tiled=True)  46.1 us
    all_gather x1, waiting for transfers between devices, body(): lax.all_gather(inputs_block, 'gx', axis=0, tiled=True)  43.9 us
    all_gather x1, waiting for transfers between devices, body(): grad_block = lax.all_gather(grad_out, 'gy', axis=1, tiled=True)  27.8 us
    all_gather x1, waiting for transfers between devices, body(): inputs_block = lax.all_gather(x_saved, 'gz', axis=1, tiled=True)  26.1 us
    dot_general x1, matrix products, body(): jnp.einsum('td,tc->dc', lax.all_gather(inputs_block, 'gx', axis=0, tiled=...  14.2 us
    dot_general x1, matrix products, body(): jnp.einsum('atc,bkc->abtk', grad_split, weight_split, preferred_element_t...  11.8 us
  transfers between devices with their start and end apart: 4, of which 4 were waited for; matrix products, arithmetic and copies ran while one was open for 10% of the time, Pallas kernels for 0%

commit v1 on v0

--- a/solution.py
+++ b/solution.py
@@ -2,6 +2,18 @@
 import jax.numpy as jnp
 from jax import lax
 from jax.sharding import PartitionSpec as P
+
+
+def settle_cube(mine_x, array_dim):
+    n_lanes = lax.axis_size("gz")
+    passed = [None] * n_lanes
+    passed[n_lanes - 1] = mine_x
+    pages = tuple(((j, (j + 1) % n_lanes) for j in range(n_lanes)))
+    for dd in range(n_lanes - 2, -1, -1):
+        passed[dd] = lax.ppermute(passed[dd + 1], "gz", pages)
+    met_up = jnp.concatenate(passed, array_dim)
+    tall = (lax.axis_index("gz") + 1) * mine_x.shape[array_dim]
+    return jnp.roll(met_up, tall, axis=array_dim)
 
 
 def body(x_saved, grad_out, weight):
@@ -11,7 +23,7 @@
     grad_block = lax.all_gather(grad_out, "gy", axis=1, tiled=True)
     grad_all = lax.all_to_all(grad_block, "gx", split_axis=1, concat_axis=0, tiled=True)
     unit_cols = grad_all.shape[1]
-    inputs_block = lax.all_gather(x_saved, "gz", axis=1, tiled=True)
+    inputs_block = settle_cube(x_saved, 1)
     summed = jnp.einsum(
         "td,tc->dc",
         lax.all_gather(inputs_block, "gx", axis=0, tiled=True),

time: 387 us -> 361 us (0.933)
  waiting for transfers between devices: 288 us -> 258 us
    all_gather x1, waiting for transfers between devices: 27.8 us -> 1.41 us  [body(): grad_block = lax.all_gather(grad_out, 'gy', axis=1, tiled=True)]
    all_gather x1 -> x0, waiting for transfers between devices: 26.1 us -> none  [body(): inputs_block = lax.all_gather(x_saved, 'gz', axis=1, tiled=True)]
    ppermute x0 -> x3, waiting for transfers between devices: none -> 23.8 us  [settle_cube(): passed[dd] = lax.ppermute(passed[dd + 1], 'gz', pages)]
  transfers between devices with their start and end apart: 4 -> 6, of which waited for: 4 -> 6; matrix products, arithmetic and copies ran while one was open for 10% -> 10% of each run, Pallas kernels for 0% -> 0%
where the time goes in v1:
time: 361 us
  waiting for transfers between devices  258 us (71%)
  blocking collectives  46.1 us (13%)
  matrix products  26 us (7%)
  between operations  13.8 us (4%)
  local copies, waits for them, and re-layouts  12.5 us (3%)
    reduce_scatter x1, waiting for transfers between devices, body(): lax.psum_scatter(terms, ('gx', 'gz'), scatter_dimension=0, tiled=True)  189 us
    all_to_all x1, blocking collectives, body(): lax.all_to_all(grad_block, 'gx', split_axis=1, concat_axis=0, tiled=True)  46.1 us
    all_gather x1, waiting for transfers between devices, body(): lax.all_gather(inputs_block, 'gx', axis=0, tiled=True)  43.9 us
    ppermute x3, waiting for transfers between devices, settle_cube(): passed[dd] = lax.ppermute(passed[dd + 1], 'gz', pages)  23.8 us
    dot_general x1, matrix products, body(): jnp.einsum('td,tc->dc', lax.all_gather(inputs_block, 'gx', axis=0, tiled=...  14.2 us
    dot_general x1, matrix products, body(): jnp.einsum('atc,bkc->abtk', grad_split, weight_split, preferred_element_t...  11.8 us
  transfers between devices with their start and end apart: 6, of which 6 were waited for; matrix products, arithmetic and copies ran while one was open for 10% of the time, Pallas kernels for 0%

profile of v1, /device:TPU:0, one launch (start us, length us, event | category | flops | bytes accessed | tf_op | source)
XLA Modules:
  0.0 360.7 jit_solution(5011906454834194043)
XLA Ops:
  7.2 0.0 copy-start.2
  7.2 0.0 all-gather.3.cloned.1.call-start
  7.2 2.0 copy.5
  9.2 0.0 all-gather.3.cloned.1.call-update
  9.3 0.0 all-gather.5.cloned.1.call-start
  9.3 1.7 collective-permute-start
  11.0 8.0 %collective-permute-done = bf16[128,1024]{1,0:T(8,128)(2,1)S(1)} collective-permute-done((bf16[128,1024]{1,0:T(8,128)(2,1)}, bf16[128,1024]{1,0:T(8,128)(2,1)S(1)}, u32[]{:S(2)}, u32[]{:S(2)}) %collective-permute-start) | collective-permute-done | bytes 262176 | tf_op jit(solution)/shard_map/ppermute | solution.py:13
  19.0 0.3 collective-permute-start.1
  19.3 8.3 %collective-permute-done.1 = bf16[128,1024]{1,0:T(8,128)(2,1)S(1)} collective-permute-done((bf16[128,1024]{1,0:T(8,128)(2,1)S(1)}, bf16[128,1024]{1,0:T(8,128)(2,1)S(1)}, u32[]{:S(2)}, u32[]{:S(2)}) %collective-permute-start.1) | collective-permute-done | bytes 262176 | tf_op jit(solution)/shard_map/ppermute | solution.py:13
  27.6 0.0 collective-permute-start.2
  27.6 7.6 %collective-permute-done.2 = bf16[128,1024]{1,0:T(8,128)(2,1)S(1)} collective-permute-done((bf16[128,1024]{1,0:T(8,128)(2,1)S(1)}, bf16[128,1024]{1,0:T(8,128)(2,1)S(1)}, u32[]{:S(2)}, u32[]{:S(2)}) %collective-permute-start.2) | collective-permute-done | bytes 262176 | tf_op jit(solution)/shard_map/ppermute | solution.py:13
  35.3 0.0 copy-done.2
  35.4 1.2 constant_dynamic-slice_fusion
  36.6 0.0 all-gather.5.cloned.1.call-update
  36.6 0.0 reduce-scatter.2.cloned.1.call-start
  36.7 1.4 all-gather.3.cloned.1.call-done
  38.1 3.1 copy.6
  41.1 46.1 %all_to_all.19 = bf16[128,8,896]{2,0,1:T(8,128)(2,1)S(1)} all-to-all(bf16[128,8,896]{2,0,1:T(8,128)(2,1)S(1)} %copy.6), channel_id=1, replica_groups=mesh['gx'=8,'gy'=4,'gz'=4] {'gx'}, dimensions={1} | all-to-all | bytes 3670016 | tf_op jit(solution)/shard_map/all_to_all | solution.py:24
  87.2 0.0 copy-start
  87.2 11.8 %convolution_bitcast_fusion = f32[8,4,128,1024]{3,2,0,1:T(8,128)S(1)} fusion(bf16[4,1024,896,1]{2,1,3,0:T(8,128)(2,1)} %bitcast.22, bf16[128,8,896]{2,0,1:T(8,128)(2,1)S(1)} %all_to_all.19), kind=kOutput, calls=%fused_computation | convolution fusion | flops 7516192768 | bytes 25952256 | tf_op jit(solution)/shard_map/atc,bkc->abtk/dot_general | solution.py:36
  99.0 0.0 copy-done
  99.0 6.1 %copy.7 = f32[8,4,128,1024]{3,2,1,0:T(8,128)} copy(f32[8,4,128,1024]{3,2,0,1:T(8,128)S(1)} %convolution_bitcast_fusion) | data formatting | bytes 33554432 | tf_op jit(solution)/shard_map/atc,bkc->abtk/transpose | solution.py:36
  105.1 0.0 copy-start.1
  105.1 0.0 reduce-scatter.2.cloned.1.call-update
  105.2 43.9 %all-gather.5.cloned.1.call-done = bf16[1024,4096]{1,0:T(8,128)(2,1)} async-done(((bf16[128,4096]{1,0:T(8,128)(2,1)}), bf16[1024,4096]{1,0:T(8,128)(2,1)}) %all-gather.5.cloned.1.call-update) | async-done | bytes 8388624 | tf_op jit(solution)/shard_map/all_gather | solution.py:29
  149.1 0.0 copy-done.1
  149.1 14.2 %convolution_convert_fusion = bf16[4096,896]{1,0:T(8,128)(2,1)} fusion(bf16[1024,4096]{1,0:T(8,128)(2,1)} %all-gather.5.cloned.1.call-done, bf16[1024,896]{1,0:T(8,128)(2,1)S(1)} %bitcast.21), kind=kOutput, calls=%fused_computation.1 | convolution fusion | flops 7519862784 | bytes 17563648 | tf_op jit(solution)/shard_map/td,tc->dc/dot_general | solution.py:27
  163.3 189.1 %reduce-scatter.2.cloned.1.call-done = f32[128,1024]{1,0:T(8,128)} async-done(((f32[4096,1024]{1,0:T(8,128)}), f32[128,1024]{1,0:T(8,128)}) %reduce-scatter.2.cloned.1.call-update) | async-done | bytes 524304 | tf_op jit(solution)/shard_map/reduce_scatter | solution.py:40
  352.4 1.8 convert_element_type.6
  (8 shorter events, 0.2 us)
Async XLA Ops:
  7.2 28.1 %copy-start.2 = (bf16[128,1024]{1,0:T(8,128)(2,1)S(1)}, bf16[128,1024]{1,0:T(8,128)(2,1)}, u32[]{:S(2)}) copy-start(bf16[128,1024]{1,0:T(8,128)(2,1)} %param.3) | copy-start | bytes 786436
  7.2 30.9 %all-gather.3.cloned.1.call-start = ((), (), s32[]{:S(2)}) async-start(), calls=%async_computation.2 | async-start | bytes 2293760 | tf_op jit(solution)/shard_map/all_gather | solution.py:23
  9.3 139.8 %all-gather.5.cloned.1.call-start = ((), (), s32[]{:S(2)}) async-start(), calls=%async_computation.4 | async-start | bytes 9437184 | tf_op jit(solution)/shard_map/all_gather | solution.py:29
  9.3 9.7 %collective-permute-start = (bf16[128,1024]{1,0:T(8,128)(2,1)}, bf16[128,1024]{1,0:T(8,128)(2,1)S(1)}, u32[]{:S(2)}, u32[]{:S(2)}) collective-permute-start(bf16[128,1024]{1,0:T(8,128)(2,1)} %param.3), channel_id=1, source_target_pairs={{0,1},{1,2},{2,3},{3,0},{4,5},{5,6},{6,7},{7,4},{8,9},{9,10},{10,1... | collective-permute-start | bytes 786440 | tf_op jit(solution)/shard_map/ppermute | solution.py:13
  19.0 8.6 %collective-permute-start.1 = (bf16[128,1024]{1,0:T(8,128)(2,1)S(1)}, bf16[128,1024]{1,0:T(8,128)(2,1)S(1)}, u32[]{:S(2)}, u32[]{:S(2)}) collective-permute-start(bf16[128,1024]{1,0:T(8,128)(2,1)S(1)} %collective-permute-done), channel_id=1, source_target_pairs={{0,1},{1,2},{2,3},{3,0},{4,5},{5,6},{6,7},{7,4},{8,9},{9,10},{10,1... | collective-permute-start | bytes 786440 | tf_op jit(solution)/shard_map/ppermute | solution.py:13
  27.6 7.6 %collective-permute-start.2 = (bf16[128,1024]{1,0:T(8,128)(2,1)S(1)}, bf16[128,1024]{1,0:T(8,128)(2,1)S(1)}, u32[]{:S(2)}, u32[]{:S(2)}) collective-permute-start(bf16[128,1024]{1,0:T(8,128)(2,1)S(1)} %collective-permute-done.1), channel_id=1, source_target_pairs={{0,1},{1,2},{2,3},{3,0},{4,5},{5,6},{6,7},{7,4},{8,9},{9,10},{10,1... | collective-permute-start | bytes 786440 | tf_op jit(solution)/shard_map/ppermute | solution.py:13
  36.6 315.8 %reduce-scatter.2.cloned.1.call-start = ((), (), s32[]{:S(2)}) async-start(), calls=%async_computation.3 | async-start | bytes 17301504 | tf_op jit(solution)/shard_map/reduce_scatter | solution.py:40
  87.2 11.8 %copy-start = (bf16[128,8,896]{2,0,1:T(8,128)(2,1)}, bf16[128,8,896]{2,0,1:T(8,128)(2,1)S(1)}, u32[]{:S(2)}) copy-start(bf16[128,8,896]{2,0,1:T(8,128)(2,1)S(1)} %all_to_all.19) | copy-start | bytes 5505028
  105.1 43.9 %copy-start.1 = (bf16[128,8,896]{2,0,1:T(8,128)(2,1)S(1)}, bf16[128,8,896]{2,0,1:T(8,128)(2,1)}, u32[]{:S(2)}) copy-start(bf16[128,8,896]{2,0,1:T(8,128)(2,1)} %copy-done) | copy-start | bytes 5505028
Sparse Core Ops, SparseCore 0:
  10.3 27.7 all-gather.2
  39.7 109.3 all-gather.4
  151.5 200.8 reduce-scatter.1
